TPU v7x, 32 devices: a whole 2x2x4 slice. The times are simulated.
32 devices in a mesh: slab: 8 (over z, core), cross: 4 (over y, x).
Axes of the slice: x: 2, y: 2, z: 4, core: 2. Of those that a mesh axis runs over, the one named last changes fastest.
Arguments:
- forcing: float32 [2, 32, 256, 512], P(None, 'slab', 'cross'), may hold values from -6 to 6
- viscosity: float32 [32, 256, 512], P('slab', 'cross'), may hold values from 0.1 to 10
- owner_slot: int32 [512], replicated, may hold values from 0 to 511, each once
Outputs:
- velocity: float32 [2, 32, 256, 512], P(None, 'slab', 'cross')
- pressure: float32 [32, 512], P('slab', 'cross')
All inputs are finite; a program needn't handle non-finite values.
Results may differ from a plain program's by a relative error of at most 0.00013.
Values sent between devices are 32-bit elements; how exact they have to be, the bound alone decides.
A program may use at most 64 MiB of HBM per device.

v0:
```python
import jax
import jax.numpy as jnp
from jax import lax
from jax.sharding import PartitionSpec as P

OUTER = 2
DEGREE = 3
cheb_theta = 1.025
cheb_delta = 0.975


def with_halo(cells, sides, width):
    for axis, dim in sides:
        count = lax.axis_size(axis)
        ends = count - 1
        head = lax.slice_in_dim(cells, 0, width, axis=dim)
        tail = lax.slice_in_dim(cells, cells.shape[dim] - width, cells.shape[dim], axis=dim)
        cells = jnp.concatenate(
            [
                lax.ppermute(tail, axis, [(i, (i + 1) % count) for i in range(ends)]),
                cells,
                lax.ppermute(head, axis, [((i + 1) % count, i) for i in range(ends)]),
            ],
            axis=dim,
        )
    return cells


def passed_along(block, axis, distance):
    devices = range(lax.axis_size(axis))
    route = [(i - distance, i) for i in devices if i - distance in devices]
    return lax.ppermute(block, axis, route)


def face_parts(viscosity):
    rim = with_halo(viscosity, (("slab", 0), ("cross", 1)), 1)
    rim = jnp.pad(rim, ((0, 0), (0, 0), (1, 1)))
    centre = rim[1:-1, 1:-1, 1:-1]
    neighbours = [
        rim[2:, 1:-1, 1:-1],
        rim[:-2, 1:-1, 1:-1],
        rim[1:-1, 2:, 1:-1],
        rim[1:-1, :-2, 1:-1],
        rim[1:-1, 1:-1, 2:],
        rim[1:-1, 1:-1, :-2],
    ]
    faces = [0.5 * (centre + nb) for nb in neighbours]
    diag = faces[0] + faces[1] + faces[2] + faces[3] + faces[4] + faces[5]
    return (faces, diag)


def apply_op(field, faces):
    padded = with_halo(field, (("slab", 1), ("cross", 2)), 1)
    padded = jnp.pad(padded, ((0, 0), (0, 0), (0, 0), (1, 1)))
    neighbours = [
        padded[:, 2:, 1:-1, 1:-1],
        padded[:, :-2, 1:-1, 1:-1],
        padded[:, 1:-1, 2:, 1:-1],
        padded[:, 1:-1, :-2, 1:-1],
        padded[:, 1:-1, 1:-1, 2:],
        padded[:, 1:-1, 1:-1, :-2],
    ]
    result = jnp.zeros_like(field)
    for face, nb in zip(faces, neighbours):
        result = result + face[None] * (field - nb)
    return result


def velocity_solve(rhs, faces, diag):
    sigma = cheb_theta / cheb_delta
    solved = rhs / (cheb_theta * diag[None])
    change = solved
    rho_prev = 1.0 / sigma
    for step in range(DEGREE - 1):
        resid = rhs - apply_op(solved, faces)
        rho = 1.0 / (2.0 * sigma - rho_prev)
        change = rho * rho_prev * change + 2.0 * rho / cheb_delta * resid / diag[None]
        solved = solved + change
        rho_prev = rho
    return solved


def diverge(field, onehot):
    col_x = jnp.sum(field[0], axis=1)
    col_z = jnp.sum(field[1], axis=1)
    prior = passed_along(col_x[-1:], "slab", 1)
    below = jnp.concatenate([prior, col_x[:-1]], 0)
    behind = jnp.pad(col_z[:, :-1], ((0, 0), (1, 0)))
    local = col_x - below + col_z - behind
    ordered = jnp.dot(local, onehot, precision=lax.Precision.HIGHEST)
    return lax.psum(ordered, "cross")


def gradient(press, onehot, ny):
    column = jnp.dot(press, onehot.T, precision=lax.Precision.HIGHEST)
    after = passed_along(column[:1], "slab", -1)
    grad_x = column - jnp.concatenate([column[1:], after], 0)
    grad_z = column - jnp.pad(column[:, 1:], ((0, 0), (0, 1)))
    both = jnp.stack([grad_x, grad_z])[:, :, None, :]
    return jnp.broadcast_to(both, (2, column.shape[0], ny, column.shape[1]))


def total(value):
    return lax.psum(value, "slab")


def shards(forcing, viscosity, owner_slot):
    faces, diag = face_parts(viscosity)
    ny = viscosity.shape[1]
    depth = owner_slot.shape[0]
    onehot = (owner_slot[:, None] == jnp.arange(depth, dtype=jnp.int32)[None, :]).astype(
        jnp.float32
    )
    target = diverge(velocity_solve(forcing, faces, diag), onehot)
    pressure = jnp.zeros_like(target)
    resid = target
    dirn = target
    rr = total(jnp.sum(resid * resid))
    for step in range(OUTER):
        image = diverge(velocity_solve(gradient(dirn, onehot, ny), faces, diag), onehot)
        alpha = rr / total(jnp.sum(dirn * image))
        pressure = pressure + alpha * dirn
        if step + 1 < OUTER:
            resid = resid - alpha * image
            fresh = total(jnp.sum(resid * resid))
            dirn = resid + fresh / rr * dirn
            rr = fresh
    velocity = velocity_solve(forcing - gradient(pressure, onehot, ny), faces, diag)
    width = depth // lax.axis_size("cross")
    owned_cols = lax.dynamic_slice_in_dim(pressure, lax.axis_index("cross") * width, width, 1)
    return (velocity, owned_cols)


def solution(mesh):
    in_specs = (P(None, "slab", "cross", None), P("slab", "cross", None), P())
    out_specs = (P(None, "slab", "cross", None), P("slab", "cross"))
    return jax.shard_map(shards, mesh=mesh, in_specs=in_specs, out_specs=out_specs, check_vma=False)
```

profile of v0, /device:TPU:12, one launch (start us, length us, event | category | flops | bytes accessed | tf_op | source)
XLA Modules:
  0.0 310.1 jit_solution(14923868998203583419)
XLA Ops:
  3.6 3.6 %collective-permute-start = (f32[1,64,512]{2,1,0:T(8,128)S(1)}, f32[1,64,512]{2,1,0:T(8,128)S(1)}, u32[]{:S(2)}, u32[]{:S(2)}) collective-permute-start(f32[1,64,512]{2,1,0:T(8,128)S(1)} %get-tuple-element.62), channel_id=1, source_target_pairs={{4,0},{8,4},{12,8},{16,12},{20,16},{24,20},{28,24},{5,1},{9,5},{13... | collective-permute-start | bytes 393224 | tf_op jit(solution)/shard_map/ppermute | solution.py:22
  15.7 4.0 %collective-permute-done.3 = f32[6,1,512]{2,1,0:T(1,128)S(1)} collective-permute-done((f32[6,1,512]{2,1,0:T(1,128)S(1)}, f32[6,1,512]{2,1,0:T(1,128)S(1)}, u32[]{:S(2)}, u32[]{:S(2)}) %collective-permute-start.3) | collective-permute-done | bytes 12320 | tf_op jit(solution)/shard_map/ppermute | solution.py:20
  28.7 3.8 %collective-permute-done.5 = f32[2,1,64,512]{3,2,1,0:T(8,128)S(1)} collective-permute-done((f32[2,1,64,512]{3,2,1,0:T(8,128)S(1)}, f32[2,1,64,512]{3,2,1,0:T(8,128)S(1)}, u32[]{:S(2)}, u32[]{:S(2)}) %collective-permute-start.5) | collective-permute-done | bytes 262176 | tf_op jit(solution)/shard_map/ppermute | solution.py:20
  34.5 3.9 %collective-permute-start.7 = (f32[2,6,1,512]{3,2,1,0:T(1,128)S(1)}, f32[2,6,1,512]{3,2,1,0:T(1,128)S(1)}, u32[]{:S(2)}, u32[]{:S(2)}) collective-permute-start(f32[2,6,1,512]{3,2,1,0:T(1,128)S(1)} %get-tuple-element.42), channel_id=1, source_target_pairs={{0,1},{1,2},{2,3},{4,5},{5,6},{6,7},{8,9},{9,10},{10,11},{12,13},{... | collective-permute-start | bytes 73736 | tf_op jit(solution)/shard_map/ppermute | solution.py:20
  49.4 3.8 %collective-permute-done.9 = f32[2,1,64,512]{3,2,1,0:T(8,128)S(1)} collective-permute-done((f32[2,1,64,512]{3,2,1,0:T(8,128)S(1)}, f32[2,1,64,512]{3,2,1,0:T(8,128)S(1)}, u32[]{:S(2)}, u32[]{:S(2)}) %collective-permute-start.9) | collective-permute-done | bytes 262176 | tf_op jit(solution)/shard_map/ppermute | solution.py:20
  55.2 3.9 %collective-permute-start.11 = (f32[2,6,1,512]{3,2,1,0:T(1,128)S(1)}, f32[2,6,1,512]{3,2,1,0:T(1,128)S(1)}, u32[]{:S(2)}, u32[]{:S(2)}) collective-permute-start(f32[2,6,1,512]{3,2,1,0:T(1,128)S(1)} %get-tuple-element.40), channel_id=1, source_target_pairs={{0,1},{1,2},{2,3},{4,5},{5,6},{6,7},{8,9},{9,10},{10,11},{12,13},{... | collective-permute-start | bytes 73736 | tf_op jit(solution)/shard_map/ppermute | solution.py:20
  70.0 8.7 %psum.49 = f32[4,512]{1,0:T(4,128)S(1)} all-reduce(f32[4,512]{1,0:T(4,128)S(1)} %fusion.163), channel_id=1, replica_groups=mesh['slab'=8,'cross'=4] {'cross'}, use_global_device_ids=true, to_apply=%region_2.3 | all-reduce | flops 2048 | bytes 16384 | tf_op jit(solution)/shard_map/psum | solution.py:91
  91.3 3.8 %collective-permute-done.15 = f32[2,1,64,512]{3,2,1,0:T(8,128)S(1)} collective-permute-done((f32[2,1,64,512]{3,2,1,0:T(8,128)S(1)}, f32[2,1,64,512]{3,2,1,0:T(8,128)S(1)}, u32[]{:S(2)}, u32[]{:S(2)}) %collective-permute-start.15) | collective-permute-done | bytes 262176 | tf_op jit(solution)/shard_map/ppermute | solution.py:20
  113.0 3.8 %collective-permute-done.19 = f32[2,1,64,512]{3,2,1,0:T(8,128)S(1)} collective-permute-done((f32[2,1,64,512]{3,2,1,0:T(8,128)S(1)}, f32[2,1,64,512]{3,2,1,0:T(8,128)S(1)}, u32[]{:S(2)}, u32[]{:S(2)}) %collective-permute-start.19) | collective-permute-done | bytes 262176 | tf_op jit(solution)/shard_map/ppermute | solution.py:20
  122.8 3.8 %collective-permute-done.21 = f32[2,6,1,512]{3,2,1,0:T(1,128)S(1)} collective-permute-done((f32[2,6,1,512]{3,2,1,0:T(1,128)S(1)}, f32[2,6,1,512]{3,2,1,0:T(1,128)S(1)}, u32[]{:S(2)}, u32[]{:S(2)}) %collective-permute-start.21) | collective-permute-done | bytes 24608 | tf_op jit(solution)/shard_map/ppermute | solution.py:20
  134.6 7.7 %psum.51 = f32[4,512]{1,0:T(4,128)S(1)} all-reduce(f32[4,512]{1,0:T(4,128)S(1)} %fusion.161), channel_id=1, replica_groups=mesh['slab'=8,'cross'=4] {'cross'}, use_global_device_ids=true, to_apply=%region_7.8 | all-reduce | flops 2048 | bytes 16384 | tf_op jit(solution)/shard_map/psum | solution.py:91
  143.0 10.6 %all-reduce.15 = (f32[]{:T(128)}, f32[]{:T(128)}) all-reduce(f32[]{:T(128)} %get-tuple-element.9, f32[]{:T(128)} %get-tuple-element.8), channel_id=1, replica_groups=mesh['slab'=8,'cross'=4] {'slab'}, use_global_device_ids=true, to_apply=%region_4.5 | all-reduce | flops 2 | bytes 16 | tf_op jit(solution)/shard_map/psum | solution.py:104
  155.5 14.3 %psum.53 = f32[]{:T(128)} all-reduce(f32[]{:T(128)} %multiply_reduce_fusion.1), channel_id=1, replica_groups=mesh['slab'=8,'cross'=4] {'slab'}, use_global_device_ids=true, to_apply=%region_11.12 | all-reduce | flops 1 | bytes 8 | tf_op jit(solution)/shard_map/psum | solution.py:104
  171.7 5.0 %collective-permute-start.23 = (f32[1,512]{1,0:T(1,128)S(1)}, f32[1,512]{1,0:T(1,128)S(1)}, u32[]{:S(2)}, u32[]{:S(2)}) collective-permute-start(f32[1,512]{1,0:T(1,128)S(1)} %slice.583), channel_id=1, source_target_pairs={{4,0},{8,4},{12,8},{16,12},{20,16},{24,20},{28,24},{5,1},{9,5},{13... | collective-permute-start | bytes 6152 | tf_op jit(solution)/shard_map/ppermute | solution.py:32
  186.7 3.8 %collective-permute-done.25 = f32[2,1,64,512]{3,2,1,0:T(8,128)S(1)} collective-permute-done((f32[2,1,64,512]{3,2,1,0:T(8,128)S(1)}, f32[2,1,64,512]{3,2,1,0:T(8,128)S(1)}, u32[]{:S(2)}, u32[]{:S(2)}) %collective-permute-start.25) | collective-permute-done | bytes 262176 | tf_op jit(solution)/shard_map/ppermute | solution.py:20
  190.6 4.1 %collective-permute-start.26 = (f32[2,6,1,512]{3,2,1,0:T(1,128)S(1)}, f32[2,6,1,512]{3,2,1,0:T(1,128)S(1)}, u32[]{:S(2)}, u32[]{:S(2)}) collective-permute-start(f32[2,6,1,512]{3,2,1,0:T(1,128)S(1)} %get-tuple-element.35), channel_id=1, source_target_pairs={{1,0},{2,1},{3,2},{5,4},{6,5},{7,6},{9,8},{10,9},{11,10},{13,12},{... | collective-permute-start | bytes 73736 | tf_op jit(solution)/shard_map/ppermute | solution.py:22
  196.6 4.7 %collective-permute-done.27 = f32[2,6,1,512]{3,2,1,0:T(1,128)S(1)} collective-permute-done((f32[2,6,1,512]{3,2,1,0:T(1,128)S(1)}, f32[2,6,1,512]{3,2,1,0:T(1,128)S(1)}, u32[]{:S(2)}, u32[]{:S(2)}) %collective-permute-start.27) | collective-permute-done | bytes 24608 | tf_op jit(solution)/shard_map/ppermute | solution.py:20
  209.6 3.8 %collective-permute-done.29 = f32[2,1,64,512]{3,2,1,0:T(8,128)S(1)} collective-permute-done((f32[2,1,64,512]{3,2,1,0:T(8,128)S(1)}, f32[2,1,64,512]{3,2,1,0:T(8,128)S(1)}, u32[]{:S(2)}, u32[]{:S(2)}) %collective-permute-start.29) | collective-permute-done | bytes 262176 | tf_op jit(solution)/shard_map/ppermute | solution.py:20
  215.5 3.8 %collective-permute-start.31 = (f32[2,6,1,512]{3,2,1,0:T(1,128)S(1)}, f32[2,6,1,512]{3,2,1,0:T(1,128)S(1)}, u32[]{:S(2)}, u32[]{:S(2)}) collective-permute-start(f32[2,6,1,512]{3,2,1,0:T(1,128)S(1)} %get-tuple-element.32), channel_id=1, source_target_pairs={{0,1},{1,2},{2,3},{4,5},{5,6},{6,7},{8,9},{9,10},{10,11},{12,13},{... | collective-permute-start | bytes 73736 | tf_op jit(solution)/shard_map/ppermute | solution.py:20
  230.1 8.6 %psum.54 = f32[4,512]{1,0:T(4,128)S(1)} all-reduce(f32[4,512]{1,0:T(4,128)S(1)} %fusion.159), channel_id=1, replica_groups=mesh['slab'=8,'cross'=4] {'cross'}, use_global_device_ids=true, to_apply=%region_14.15 | all-reduce | flops 2048 | bytes 16384 | tf_op jit(solution)/shard_map/psum | solution.py:91
  239.4 11.2 %psum.55 = f32[]{:T(128)} all-reduce(f32[]{:T(128)} %multiply_reduce_fusion), channel_id=1, replica_groups=mesh['slab'=8,'cross'=4] {'slab'}, use_global_device_ids=true, to_apply=%region_16.17 | all-reduce | flops 1 | bytes 8 | tf_op jit(solution)/shard_map/psum | solution.py:104
  265.4 3.8 %collective-permute-done.35 = f32[2,1,64,512]{3,2,1,0:T(8,128)S(1)} collective-permute-done((f32[2,1,64,512]{3,2,1,0:T(8,128)S(1)}, f32[2,1,64,512]{3,2,1,0:T(8,128)S(1)}, u32[]{:S(2)}, u32[]{:S(2)}) %collective-permute-start.35) | collective-permute-done | bytes 262176 | tf_op jit(solution)/shard_map/ppermute | solution.py:20
  275.3 3.7 %collective-permute-done.37 = f32[2,6,1,512]{3,2,1,0:T(1,128)S(1)} collective-permute-done((f32[2,6,1,512]{3,2,1,0:T(1,128)S(1)}, f32[2,6,1,512]{3,2,1,0:T(1,128)S(1)}, u32[]{:S(2)}, u32[]{:S(2)}) %collective-permute-start.37) | collective-permute-done | bytes 24608 | tf_op jit(solution)/shard_map/ppermute | solution.py:20
  290.2 3.8 %collective-permute-done.39 = f32[2,1,64,512]{3,2,1,0:T(8,128)} collective-permute-done((f32[2,1,64,512]{3,2,1,0:T(8,128)}, f32[2,1,64,512]{3,2,1,0:T(8,128)}, u32[]{:S(2)}, u32[]{:S(2)}) %collective-permute-start.39) | collective-permute-done | bytes 262176 | tf_op jit(solution)/shard_map/ppermute | solution.py:20
  (174 shorter events, 172.3 us)
Async XLA Ops:
  1.7 6.3 %collective-permute-start.1 = (f32[1,64,512]{2,1,0:T(8,128)S(1)}, f32[1,64,512]{2,1,0:T(8,128)S(1)}, u32[]{:S(2)}, u32[]{:S(2)}) collective-permute-start(f32[1,64,512]{2,1,0:T(8,128)S(1)} %get-tuple-element.63), channel_id=1, source_target_pairs={{0,4},{4,8},{8,12},{12,16},{16,20},{20,24},{24,28},{1,5},{5,9},{9,... | collective-permute-start | bytes 393224 | tf_op jit(solution)/shard_map/ppermute | solution.py:20
  13.2 6.5 %collective-permute-start.3 = (f32[6,1,512]{2,1,0:T(1,128)S(1)}, f32[6,1,512]{2,1,0:T(1,128)S(1)}, u32[]{:S(2)}, u32[]{:S(2)}) collective-permute-start(f32[6,1,512]{2,1,0:T(1,128)S(1)} %get-tuple-element.60), channel_id=1, source_target_pairs={{0,1},{1,2},{2,3},{4,5},{5,6},{6,7},{8,9},{9,10},{10,11},{12,13},{... | collective-permute-start | bytes 36872 | tf_op jit(solution)/shard_map/ppermute | solution.py:20
  22.4 6.2 %collective-permute-start.4 = (f32[2,1,64,512]{3,2,1,0:T(8,128)S(1)}, f32[2,1,64,512]{3,2,1,0:T(8,128)S(1)}, u32[]{:S(2)}, u32[]{:S(2)}) collective-permute-start(f32[2,1,64,512]{3,2,1,0:T(8,128)S(1)} %get-tuple-element.59), channel_id=1, source_target_pairs={{4,0},{8,4},{12,8},{16,12},{20,16},{24,20},{28,24},{5,1},{9,5},{13... | collective-permute-start | bytes 786440 | tf_op jit(solution)/shard_map/ppermute | solution.py:22
  24.8 7.7 %collective-permute-start.5 = (f32[2,1,64,512]{3,2,1,0:T(8,128)S(1)}, f32[2,1,64,512]{3,2,1,0:T(8,128)S(1)}, u32[]{:S(2)}, u32[]{:S(2)}) collective-permute-start(f32[2,1,64,512]{3,2,1,0:T(8,128)S(1)} %get-tuple-element.58), channel_id=1, source_target_pairs={{0,4},{4,8},{8,12},{12,16},{16,20},{20,24},{24,28},{1,5},{5,9},{9,... | collective-permute-start | bytes 786440 | tf_op jit(solution)/shard_map/ppermute | solution.py:20
  34.5 6.6 %collective-permute-start.7 = (f32[2,6,1,512]{3,2,1,0:T(1,128)S(1)}, f32[2,6,1,512]{3,2,1,0:T(1,128)S(1)}, u32[]{:S(2)}, u32[]{:S(2)}) collective-permute-start(f32[2,6,1,512]{3,2,1,0:T(1,128)S(1)} %get-tuple-element.42), channel_id=1, source_target_pairs={{0,1},{1,2},{2,3},{4,5},{5,6},{6,7},{8,9},{9,10},{10,11},{12,13},{... | collective-permute-start | bytes 73736 | tf_op jit(solution)/shard_map/ppermute | solution.py:20
  45.5 7.7 %collective-permute-start.9 = (f32[2,1,64,512]{3,2,1,0:T(8,128)S(1)}, f32[2,1,64,512]{3,2,1,0:T(8,128)S(1)}, u32[]{:S(2)}, u32[]{:S(2)}) collective-permute-start(f32[2,1,64,512]{3,2,1,0:T(8,128)S(1)} %get-tuple-element.56), channel_id=1, source_target_pairs={{0,4},{4,8},{8,12},{12,16},{16,20},{20,24},{24,28},{1,5},{5,9},{9,... | collective-permute-start | bytes 786440 | tf_op jit(solution)/shard_map/ppermute | solution.py:20
  55.2 6.6 %collective-permute-start.11 = (f32[2,6,1,512]{3,2,1,0:T(1,128)S(1)}, f32[2,6,1,512]{3,2,1,0:T(1,128)S(1)}, u32[]{:S(2)}, u32[]{:S(2)}) collective-permute-start(f32[2,6,1,512]{3,2,1,0:T(1,128)S(1)} %get-tuple-element.40), channel_id=1, source_target_pairs={{0,1},{1,2},{2,3},{4,5},{5,6},{6,7},{8,9},{9,10},{10,11},{12,13},{... | collective-permute-start | bytes 73736 | tf_op jit(solution)/shard_map/ppermute | solution.py:20
  83.8 7.5 %collective-permute-start.14 = (f32[2,1,64,512]{3,2,1,0:T(8,128)S(1)}, f32[2,1,64,512]{3,2,1,0:T(8,128)S(1)}, u32[]{:S(2)}, u32[]{:S(2)}) collective-permute-start(f32[2,1,64,512]{3,2,1,0:T(8,128)S(1)} %get-tuple-element.55), channel_id=1, source_target_pairs={{4,0},{8,4},{12,8},{16,12},{20,16},{24,20},{28,24},{5,1},{9,5},{13... | collective-permute-start | bytes 786440 | tf_op jit(solution)/shard_map/ppermute | solution.py:22
  87.4 7.7 %collective-permute-start.15 = (f32[2,1,64,512]{3,2,1,0:T(8,128)S(1)}, f32[2,1,64,512]{3,2,1,0:T(8,128)S(1)}, u32[]{:S(2)}, u32[]{:S(2)}) collective-permute-start(f32[2,1,64,512]{3,2,1,0:T(8,128)S(1)} %get-tuple-element.54), channel_id=1, source_target_pairs={{0,4},{4,8},{8,12},{12,16},{16,20},{20,24},{24,28},{1,5},{5,9},{9,... | collective-permute-start | bytes 786440 | tf_op jit(solution)/shard_map/ppermute | solution.py:20
  98.1 6.6 %collective-permute-start.17 = (f32[2,6,1,512]{3,2,1,0:T(1,128)S(1)}, f32[2,6,1,512]{3,2,1,0:T(1,128)S(1)}, u32[]{:S(2)}, u32[]{:S(2)}) collective-permute-start(f32[2,6,1,512]{3,2,1,0:T(1,128)S(1)} %get-tuple-element.38), channel_id=1, source_target_pairs={{0,1},{1,2},{2,3},{4,5},{5,6},{6,7},{8,9},{9,10},{10,11},{12,13},{... | collective-permute-start | bytes 73736 | tf_op jit(solution)/shard_map/ppermute | solution.py:20
  109.2 7.7 %collective-permute-start.19 = (f32[2,1,64,512]{3,2,1,0:T(8,128)S(1)}, f32[2,1,64,512]{3,2,1,0:T(8,128)S(1)}, u32[]{:S(2)}, u32[]{:S(2)}) collective-permute-start(f32[2,1,64,512]{3,2,1,0:T(8,128)S(1)} %get-tuple-element.52), channel_id=1, source_target_pairs={{0,4},{4,8},{8,12},{12,16},{16,20},{20,24},{24,28},{1,5},{5,9},{9,... | collective-permute-start | bytes 786440 | tf_op jit(solution)/shard_map/ppermute | solution.py:20
  119.9 6.6 %collective-permute-start.21 = (f32[2,6,1,512]{3,2,1,0:T(1,128)S(1)}, f32[2,6,1,512]{3,2,1,0:T(1,128)S(1)}, u32[]{:S(2)}, u32[]{:S(2)}) collective-permute-start(f32[2,6,1,512]{3,2,1,0:T(1,128)S(1)} %get-tuple-element.36), channel_id=1, source_target_pairs={{0,1},{1,2},{2,3},{4,5},{5,6},{6,7},{8,9},{9,10},{10,11},{12,13},{... | collective-permute-start | bytes 73736 | tf_op jit(solution)/shard_map/ppermute | solution.py:20
  171.7 6.3 %collective-permute-start.23 = (f32[1,512]{1,0:T(1,128)S(1)}, f32[1,512]{1,0:T(1,128)S(1)}, u32[]{:S(2)}, u32[]{:S(2)}) collective-permute-start(f32[1,512]{1,0:T(1,128)S(1)} %slice.583), channel_id=1, source_target_pairs={{4,0},{8,4},{12,8},{16,12},{20,16},{24,20},{28,24},{5,1},{9,5},{13... | collective-permute-start | bytes 6152 | tf_op jit(solution)/shard_map/ppermute | solution.py:32
  179.2 7.5 %collective-permute-start.24 = (f32[2,1,64,512]{3,2,1,0:T(8,128)S(1)}, f32[2,1,64,512]{3,2,1,0:T(8,128)S(1)}, u32[]{:S(2)}, u32[]{:S(2)}) collective-permute-start(f32[2,1,64,512]{3,2,1,0:T(8,128)S(1)} %get-tuple-element.51), channel_id=1, source_target_pairs={{4,0},{8,4},{12,8},{16,12},{20,16},{24,20},{28,24},{5,1},{9,5},{13... | collective-permute-start | bytes 786440 | tf_op jit(solution)/shard_map/ppermute | solution.py:22
  182.9 7.7 %collective-permute-start.25 = (f32[2,1,64,512]{3,2,1,0:T(8,128)S(1)}, f32[2,1,64,512]{3,2,1,0:T(8,128)S(1)}, u32[]{:S(2)}, u32[]{:S(2)}) collective-permute-start(f32[2,1,64,512]{3,2,1,0:T(8,128)S(1)} %get-tuple-element.50), channel_id=1, source_target_pairs={{0,4},{4,8},{8,12},{12,16},{16,20},{20,24},{24,28},{1,5},{5,9},{9,... | collective-permute-start | bytes 786440 | tf_op jit(solution)/shard_map/ppermute | solution.py:20
  194.7 6.6 %collective-permute-start.27 = (f32[2,6,1,512]{3,2,1,0:T(1,128)S(1)}, f32[2,6,1,512]{3,2,1,0:T(1,128)S(1)}, u32[]{:S(2)}, u32[]{:S(2)}) collective-permute-start(f32[2,6,1,512]{3,2,1,0:T(1,128)S(1)} %get-tuple-element.34), channel_id=1, source_target_pairs={{0,1},{1,2},{2,3},{4,5},{5,6},{6,7},{8,9},{9,10},{10,11},{12,13},{... | collective-permute-start | bytes 73736 | tf_op jit(solution)/shard_map/ppermute | solution.py:20
  205.7 7.7 %collective-permute-start.29 = (f32[2,1,64,512]{3,2,1,0:T(8,128)S(1)}, f32[2,1,64,512]{3,2,1,0:T(8,128)S(1)}, u32[]{:S(2)}, u32[]{:S(2)}) collective-permute-start(f32[2,1,64,512]{3,2,1,0:T(8,128)S(1)} %get-tuple-element.48), channel_id=1, source_target_pairs={{0,4},{4,8},{8,12},{12,16},{16,20},{20,24},{24,28},{1,5},{5,9},{9,... | collective-permute-start | bytes 786440 | tf_op jit(solution)/shard_map/ppermute | solution.py:20
  215.5 6.6 %collective-permute-start.31 = (f32[2,6,1,512]{3,2,1,0:T(1,128)S(1)}, f32[2,6,1,512]{3,2,1,0:T(1,128)S(1)}, u32[]{:S(2)}, u32[]{:S(2)}) collective-permute-start(f32[2,6,1,512]{3,2,1,0:T(1,128)S(1)} %get-tuple-element.32), channel_id=1, source_target_pairs={{0,1},{1,2},{2,3},{4,5},{5,6},{6,7},{8,9},{9,10},{10,11},{12,13},{... | collective-permute-start | bytes 73736 | tf_op jit(solution)/shard_map/ppermute | solution.py:20
  257.9 7.5 %collective-permute-start.34 = (f32[2,1,64,512]{3,2,1,0:T(8,128)S(1)}, f32[2,1,64,512]{3,2,1,0:T(8,128)S(1)}, u32[]{:S(2)}, u32[]{:S(2)}) collective-permute-start(f32[2,1,64,512]{3,2,1,0:T(8,128)S(1)} %get-tuple-element.47), channel_id=1, source_target_pairs={{4,0},{8,4},{12,8},{16,12},{20,16},{24,20},{28,24},{5,1},{9,5},{13... | collective-permute-start | bytes 786440 | tf_op jit(solution)/shard_map/ppermute | solution.py:22
  261.5 7.7 %collective-permute-start.35 = (f32[2,1,64,512]{3,2,1,0:T(8,128)S(1)}, f32[2,1,64,512]{3,2,1,0:T(8,128)S(1)}, u32[]{:S(2)}, u32[]{:S(2)}) collective-permute-start(f32[2,1,64,512]{3,2,1,0:T(8,128)S(1)} %get-tuple-element.46), channel_id=1, source_target_pairs={{0,4},{4,8},{8,12},{12,16},{16,20},{20,24},{24,28},{1,5},{5,9},{9,... | collective-permute-start | bytes 786440 | tf_op jit(solution)/shard_map/ppermute | solution.py:20
  272.3 6.6 %collective-permute-start.37 = (f32[2,6,1,512]{3,2,1,0:T(1,128)S(1)}, f32[2,6,1,512]{3,2,1,0:T(1,128)S(1)}, u32[]{:S(2)}, u32[]{:S(2)}) collective-permute-start(f32[2,6,1,512]{3,2,1,0:T(1,128)S(1)} %get-tuple-element.30), channel_id=1, source_target_pairs={{0,1},{1,2},{2,3},{4,5},{5,6},{6,7},{8,9},{9,10},{10,11},{12,13},{... | collective-permute-start | bytes 73736 | tf_op jit(solution)/shard_map/ppermute | solution.py:20
  286.0 8.0 %collective-permute-start.39 = (f32[2,1,64,512]{3,2,1,0:T(8,128)}, f32[2,1,64,512]{3,2,1,0:T(8,128)}, u32[]{:S(2)}, u32[]{:S(2)}) collective-permute-start(f32[2,1,64,512]{3,2,1,0:T(8,128)} %get-tuple-element.44), channel_id=1, source_target_pairs={{0,4},{4,8},{8,12},{12,16},{16,20},{20,24},{24,28},{1,5},{5,9},{9,... | collective-permute-start | bytes 786440 | tf_op jit(solution)/shard_map/ppermute | solution.py:20
  295.1 6.6 %collective-permute-start.40 = (f32[2,6,1,512]{3,2,1,0:T(1,128)S(1)}, f32[2,6,1,512]{3,2,1,0:T(1,128)S(1)}, u32[]{:S(2)}, u32[]{:S(2)}) collective-permute-start(f32[2,6,1,512]{3,2,1,0:T(1,128)S(1)} %get-tuple-element.29), channel_id=1, source_target_pairs={{1,0},{2,1},{3,2},{5,4},{6,5},{7,6},{9,8},{10,9},{11,10},{13,12},{... | collective-permute-start | bytes 73736 | tf_op jit(solution)/shard_map/ppermute | solution.py:22
  298.1 6.6 %collective-permute-start.41 = (f32[2,6,1,512]{3,2,1,0:T(1,128)S(1)}, f32[2,6,1,512]{3,2,1,0:T(1,128)S(1)}, u32[]{:S(2)}, u32[]{:S(2)}) collective-permute-start(f32[2,6,1,512]{3,2,1,0:T(1,128)S(1)} %get-tuple-element.28), channel_id=1, source_target_pairs={{0,1},{1,2},{2,3},{4,5},{5,6},{6,7},{8,9},{9,10},{10,11},{12,13},{... | collective-permute-start | bytes 73736 | tf_op jit(solution)/shard_map/ppermute | solution.py:20
  (34 other events, 295.4 us)
where the time goes:
time: 312 us; the launch traced here: 310 us
  starting transfers between devices  112 us (36%)
  waiting for transfers between devices  89.3 us (29%)
  blocking collectives  61.2 us (20%)
  other arithmetic  32.4 us (10%)
  local copies, waits for them, and re-layouts  6.4 us (2%)
  between operations  5.48 us (2%)
  matrix products  3.36 us (1%)
    ppermute x18, waiting for transfers between devices, with_halo(): lax.ppermute(tail, axis, [(i, (i + 1) % count) for i in range(ends)])  62.2 us
    ppermute x18, starting transfers between devices, with_halo(): lax.ppermute(head, axis, [((i + 1) % count, i) for i in range(ends)])  49.8 us
    ppermute x18, starting transfers between devices, with_halo(): lax.ppermute(tail, axis, [(i, (i + 1) % count) for i in range(ends)])  47 us
    psum x3, blocking collectives, total(): return lax.psum(value, 'slab')  36.2 us
    psum x3, blocking collectives, diverge(): return lax.psum(ordered, 'cross')  25.1 us
    add x8, other arithmetic, velocity_solve(): solved = solved + change  15.6 us
    ppermute x6, starting transfers between devices, passed_along(): return lax.ppermute(block, axis, route)  15.1 us
    ppermute x18, waiting for transfers between devices, with_halo(): lax.ppermute(head, axis, [((i + 1) % count, i) for i in range(ends)])  14.5 us
  transfers between devices with their start and end apart: 42, of which 33 were waited for; matrix products, arithmetic and copies ran while one was open for 1% of the time, Pallas kernels for 0%

commit v1 on v0

--- a/solution.py
+++ b/solution.py
@@ -88,7 +88,7 @@
     behind = jnp.pad(col_z[:, :-1], ((0, 0), (1, 0)))
     local = col_x - below + col_z - behind
     ordered = jnp.dot(local, onehot, precision=lax.Precision.HIGHEST)
-    return lax.psum(ordered, "cross")
+    return jnp.sum(lax.all_gather(ordered, "cross"), axis=0)
 
 
 def gradient(press, onehot, ny):

time: 312 us -> 308 us (0.987)
    psum x3 -> x0, blocking collectives: 25.1 us -> none  [diverge(): return lax.psum(ordered, 'cross')]
    all_gather x0 -> x3, blocking collectives: none -> 23.3 us  [diverge(): return jnp.sum(lax.all_gather(ordered, 'cross'), axis=0)]
where the time goes in v1:
time: 308 us; the launch traced here: 307 us
  starting transfers between devices  112 us (36%)
  waiting for transfers between devices  87.4 us (28%)
  blocking collectives  59.5 us (19%)
  other arithmetic  32.4 us (11%)
  local copies, waits for them, and re-layouts  6.4 us (2%)
  between operations  5.47 us (2%)
  matrix products  3.36 us (1%)
    ppermute x18, waiting for transfers between devices, with_halo(): lax.ppermute(tail, axis, [(i, (i + 1) % count) for i in range(ends)])  60.5 us
    ppermute x18, starting transfers between devices, with_halo(): lax.ppermute(tail, axis, [(i, (i + 1) % count) for i in range(ends)])  48.7 us
    ppermute x18, starting transfers between devices, with_halo(): lax.ppermute(head, axis, [((i + 1) % count, i) for i in range(ends)])  48.1 us
    psum x3, blocking collectives, total(): return lax.psum(value, 'slab')  36.2 us
    all_gather x3, blocking collectives, diverge(): return jnp.sum(lax.all_gather(ordered, 'cross'), axis=0)  23.3 us
    add x8, other arithmetic, velocity_solve(): solved = solved + change  15.6 us
    ppermute x6, starting transfers between devices, passed_along(): return lax.ppermute(block, axis, route)  15.3 us
    ppermute x18, waiting for transfers between devices, with_halo(): lax.ppermute(head, axis, [((i + 1) % count, i) for i in range(ends)])  14.5 us
  transfers between devices with their start and end apart: 42, of which 33 were waited for; matrix products, arithmetic and copies ran while one was open for 1% of the time, Pallas kernels for 0%

profile of v1, /device:TPU:12, one launch (start us, length us, event | category | flops | bytes accessed | tf_op | source)
XLA Modules:
  0.0 306.7 jit_solution(4125909231881144252)
XLA Ops:
  15.7 4.0 %collective-permute-done.3 = f32[6,1,512]{2,1,0:T(1,128)S(1)} collective-permute-done((f32[6,1,512]{2,1,0:T(1,128)S(1)}, f32[6,1,512]{2,1,0:T(1,128)S(1)}, u32[]{:S(2)}, u32[]{:S(2)}) %collective-permute-start.3) | collective-permute-done | bytes 12320 | tf_op jit(solution)/shard_map/ppermute | solution.py:20
  28.7 3.8 %collective-permute-done.5 = f32[2,1,64,512]{3,2,1,0:T(8,128)S(1)} collective-permute-done((f32[2,1,64,512]{3,2,1,0:T(8,128)S(1)}, f32[2,1,64,512]{3,2,1,0:T(8,128)S(1)}, u32[]{:S(2)}, u32[]{:S(2)}) %collective-permute-start.5) | collective-permute-done | bytes 262176 | tf_op jit(solution)/shard_map/ppermute | solution.py:20
  34.5 3.9 %collective-permute-start.7 = (f32[2,6,1,512]{3,2,1,0:T(1,128)S(1)}, f32[2,6,1,512]{3,2,1,0:T(1,128)S(1)}, u32[]{:S(2)}, u32[]{:S(2)}) collective-permute-start(f32[2,6,1,512]{3,2,1,0:T(1,128)S(1)} %get-tuple-element.42), channel_id=1, source_target_pairs={{0,1},{1,2},{2,3},{4,5},{5,6},{6,7},{8,9},{9,10},{10,11},{12,13},{... | collective-permute-start | bytes 73736 | tf_op jit(solution)/shard_map/ppermute | solution.py:20
  49.4 3.8 %collective-permute-done.9 = f32[2,1,64,512]{3,2,1,0:T(8,128)S(1)} collective-permute-done((f32[2,1,64,512]{3,2,1,0:T(8,128)S(1)}, f32[2,1,64,512]{3,2,1,0:T(8,128)S(1)}, u32[]{:S(2)}, u32[]{:S(2)}) %collective-permute-start.9) | collective-permute-done | bytes 262176 | tf_op jit(solution)/shard_map/ppermute | solution.py:20
  55.2 3.9 %collective-permute-start.11 = (f32[2,6,1,512]{3,2,1,0:T(1,128)S(1)}, f32[2,6,1,512]{3,2,1,0:T(1,128)S(1)}, u32[]{:S(2)}, u32[]{:S(2)}) collective-permute-start(f32[2,6,1,512]{3,2,1,0:T(1,128)S(1)} %get-tuple-element.40), channel_id=1, source_target_pairs={{0,1},{1,2},{2,3},{4,5},{5,6},{6,7},{8,9},{9,10},{10,11},{12,13},{... | collective-permute-start | bytes 73736 | tf_op jit(solution)/shard_map/ppermute | solution.py:20
  70.0 7.8 %all-gather.3 = f32[4,4,512]{2,1,0:T(4,128)S(1)} all-gather(f32[1,4,512]{2,1,0:T(4,128)S(1)} %convolution_bitcast_fusion.2), channel_id=2, replica_groups=mesh['slab'=8,'cross'=4] {'cross'}, dimensions={0}, use_global_device_ids=true | all-gather | bytes 40960 | tf_op jit(solution)/shard_map/all_gather | solution.py:91
  90.4 3.8 %collective-permute-done.15 = f32[2,1,64,512]{3,2,1,0:T(8,128)S(1)} collective-permute-done((f32[2,1,64,512]{3,2,1,0:T(8,128)S(1)}, f32[2,1,64,512]{3,2,1,0:T(8,128)S(1)}, u32[]{:S(2)}, u32[]{:S(2)}) %collective-permute-start.15) | collective-permute-done | bytes 262176 | tf_op jit(solution)/shard_map/ppermute | solution.py:20
  100.2 4.1 %collective-permute-done.17 = f32[2,6,1,512]{3,2,1,0:T(1,128)S(1)} collective-permute-done((f32[2,6,1,512]{3,2,1,0:T(1,128)S(1)}, f32[2,6,1,512]{3,2,1,0:T(1,128)S(1)}, u32[]{:S(2)}, u32[]{:S(2)}) %collective-permute-start.17) | collective-permute-done | bytes 24608 | tf_op jit(solution)/shard_map/ppermute | solution.py:20
  112.7 3.8 %collective-permute-done.19 = f32[2,1,64,512]{3,2,1,0:T(8,128)S(1)} collective-permute-done((f32[2,1,64,512]{3,2,1,0:T(8,128)S(1)}, f32[2,1,64,512]{3,2,1,0:T(8,128)S(1)}, u32[]{:S(2)}, u32[]{:S(2)}) %collective-permute-start.19) | collective-permute-done | bytes 262176 | tf_op jit(solution)/shard_map/ppermute | solution.py:20
  118.5 3.9 %collective-permute-start.21 = (f32[2,6,1,512]{3,2,1,0:T(1,128)S(1)}, f32[2,6,1,512]{3,2,1,0:T(1,128)S(1)}, u32[]{:S(2)}, u32[]{:S(2)}) collective-permute-start(f32[2,6,1,512]{3,2,1,0:T(1,128)S(1)} %get-tuple-element.36), channel_id=1, source_target_pairs={{0,1},{1,2},{2,3},{4,5},{5,6},{6,7},{8,9},{9,10},{10,11},{12,13},{... | collective-permute-start | bytes 73736 | tf_op jit(solution)/shard_map/ppermute | solution.py:20
  133.1 7.8 %all-gather.4 = f32[4,4,512]{2,1,0:T(4,128)S(1)} all-gather(f32[1,4,512]{2,1,0:T(4,128)S(1)} %convolution_bitcast_fusion.1), channel_id=3, replica_groups=mesh['slab'=8,'cross'=4] {'cross'}, dimensions={0}, use_global_device_ids=true | all-gather | bytes 40960 | tf_op jit(solution)/shard_map/all_gather | solution.py:91
  141.6 10.6 %all-reduce.15 = (f32[]{:T(128)}, f32[]{:T(128)}) all-reduce(f32[]{:T(128)} %get-tuple-element.9, f32[]{:T(128)} %get-tuple-element.8), channel_id=1, replica_groups=mesh['slab'=8,'cross'=4] {'slab'}, use_global_device_ids=true, to_apply=%region_4.5 | all-reduce | flops 2 | bytes 16 | tf_op jit(solution)/shard_map/psum | solution.py:104
  154.1 14.3 %psum.30 = f32[]{:T(128)} all-reduce(f32[]{:T(128)} %multiply_reduce_fusion.1), channel_id=1, replica_groups=mesh['slab'=8,'cross'=4] {'slab'}, use_global_device_ids=true, to_apply=%region_11.12 | all-reduce | flops 1 | bytes 8 | tf_op jit(solution)/shard_map/psum | solution.py:104
  170.3 5.0 %collective-permute-start.23 = (f32[1,512]{1,0:T(1,128)S(1)}, f32[1,512]{1,0:T(1,128)S(1)}, u32[]{:S(2)}, u32[]{:S(2)}) collective-permute-start(f32[1,512]{1,0:T(1,128)S(1)} %slice.583), channel_id=1, source_target_pairs={{4,0},{8,4},{12,8},{16,12},{20,16},{24,20},{28,24},{5,1},{9,5},{13... | collective-permute-start | bytes 6152 | tf_op jit(solution)/shard_map/ppermute | solution.py:32
  185.3 3.8 %collective-permute-done.25 = f32[2,1,64,512]{3,2,1,0:T(8,128)S(1)} collective-permute-done((f32[2,1,64,512]{3,2,1,0:T(8,128)S(1)}, f32[2,1,64,512]{3,2,1,0:T(8,128)S(1)}, u32[]{:S(2)}, u32[]{:S(2)}) %collective-permute-start.25) | collective-permute-done | bytes 262176 | tf_op jit(solution)/shard_map/ppermute | solution.py:20
  195.2 4.1 %collective-permute-done.27 = f32[2,6,1,512]{3,2,1,0:T(1,128)S(1)} collective-permute-done((f32[2,6,1,512]{3,2,1,0:T(1,128)S(1)}, f32[2,6,1,512]{3,2,1,0:T(1,128)S(1)}, u32[]{:S(2)}, u32[]{:S(2)}) %collective-permute-start.27) | collective-permute-done | bytes 24608 | tf_op jit(solution)/shard_map/ppermute | solution.py:20
  207.6 3.8 %collective-permute-done.29 = f32[2,1,64,512]{3,2,1,0:T(8,128)S(1)} collective-permute-done((f32[2,1,64,512]{3,2,1,0:T(8,128)S(1)}, f32[2,1,64,512]{3,2,1,0:T(8,128)S(1)}, u32[]{:S(2)}, u32[]{:S(2)}) %collective-permute-start.29) | collective-permute-done | bytes 262176 | tf_op jit(solution)/shard_map/ppermute | solution.py:20
  213.4 3.9 %collective-permute-start.31 = (f32[2,6,1,512]{3,2,1,0:T(1,128)S(1)}, f32[2,6,1,512]{3,2,1,0:T(1,128)S(1)}, u32[]{:S(2)}, u32[]{:S(2)}) collective-permute-start(f32[2,6,1,512]{3,2,1,0:T(1,128)S(1)} %get-tuple-element.32), channel_id=1, source_target_pairs={{0,1},{1,2},{2,3},{4,5},{5,6},{6,7},{8,9},{9,10},{10,11},{12,13},{... | collective-permute-start | bytes 73736 | tf_op jit(solution)/shard_map/ppermute | solution.py:20
  228.1 7.8 %all-gather.5 = f32[4,4,512]{2,1,0:T(4,128)S(1)} all-gather(f32[1,4,512]{2,1,0:T(4,128)S(1)} %convolution_bitcast_fusion), channel_id=4, replica_groups=mesh['slab'=8,'cross'=4] {'cross'}, dimensions={0}, use_global_device_ids=true | all-gather | bytes 40960 | tf_op jit(solution)/shard_map/all_gather | solution.py:91
  236.5 11.2 %psum.31 = f32[]{:T(128)} all-reduce(f32[]{:T(128)} %multiply_reduce_fusion), channel_id=1, replica_groups=mesh['slab'=8,'cross'=4] {'slab'}, use_global_device_ids=true, to_apply=%region_16.17 | all-reduce | flops 1 | bytes 8 | tf_op jit(solution)/shard_map/psum | solution.py:104
  262.5 3.8 %collective-permute-done.35 = f32[2,1,64,512]{3,2,1,0:T(8,128)S(1)} collective-permute-done((f32[2,1,64,512]{3,2,1,0:T(8,128)S(1)}, f32[2,1,64,512]{3,2,1,0:T(8,128)S(1)}, u32[]{:S(2)}, u32[]{:S(2)}) %collective-permute-start.35) | collective-permute-done | bytes 262176 | tf_op jit(solution)/shard_map/ppermute | solution.py:20
  272.4 4.1 %collective-permute-done.37 = f32[2,6,1,512]{3,2,1,0:T(1,128)S(1)} collective-permute-done((f32[2,6,1,512]{3,2,1,0:T(1,128)S(1)}, f32[2,6,1,512]{3,2,1,0:T(1,128)S(1)}, u32[]{:S(2)}, u32[]{:S(2)}) %collective-permute-start.37) | collective-permute-done | bytes 24608 | tf_op jit(solution)/shard_map/ppermute | solution.py:20
  287.8 3.8 %collective-permute-done.39 = f32[2,1,64,512]{3,2,1,0:T(8,128)} collective-permute-done((f32[2,1,64,512]{3,2,1,0:T(8,128)}, f32[2,1,64,512]{3,2,1,0:T(8,128)}, u32[]{:S(2)}, u32[]{:S(2)}) %collective-permute-start.39) | collective-permute-done | bytes 262176 | tf_op jit(solution)/shard_map/ppermute | solution.py:20
  294.7 3.9 %collective-permute-start.41 = (f32[2,6,1,512]{3,2,1,0:T(1,128)S(1)}, f32[2,6,1,512]{3,2,1,0:T(1,128)S(1)}, u32[]{:S(2)}, u32[]{:S(2)}) collective-permute-start(f32[2,6,1,512]{3,2,1,0:T(1,128)S(1)} %get-tuple-element.28), channel_id=1, source_target_pairs={{0,1},{1,2},{2,3},{4,5},{5,6},{6,7},{8,9},{9,10},{10,11},{12,13},{... | collective-permute-start | bytes 73736 | tf_op jit(solution)/shard_map/ppermute | solution.py:20
  (177 shorter events, 170.2 us)
Async XLA Ops:
  1.7 6.3 %collective-permute-start.1 = (f32[1,64,512]{2,1,0:T(8,128)S(1)}, f32[1,64,512]{2,1,0:T(8,128)S(1)}, u32[]{:S(2)}, u32[]{:S(2)}) collective-permute-start(f32[1,64,512]{2,1,0:T(8,128)S(1)} %get-tuple-element.63), channel_id=1, source_target_pairs={{0,4},{4,8},{8,12},{12,16},{16,20},{20,24},{24,28},{1,5},{5,9},{9,... | collective-permute-start | bytes 393224 | tf_op jit(solution)/shard_map/ppermute | solution.py:20
  13.2 6.5 %collective-permute-start.3 = (f32[6,1,512]{2,1,0:T(1,128)S(1)}, f32[6,1,512]{2,1,0:T(1,128)S(1)}, u32[]{:S(2)}, u32[]{:S(2)}) collective-permute-start(f32[6,1,512]{2,1,0:T(1,128)S(1)} %get-tuple-element.60), channel_id=1, source_target_pairs={{0,1},{1,2},{2,3},{4,5},{5,6},{6,7},{8,9},{9,10},{10,11},{12,13},{... | collective-permute-start | bytes 36872 | tf_op jit(solution)/shard_map/ppermute | solution.py:20
  22.4 6.2 %collective-permute-start.4 = (f32[2,1,64,512]{3,2,1,0:T(8,128)S(1)}, f32[2,1,64,512]{3,2,1,0:T(8,128)S(1)}, u32[]{:S(2)}, u32[]{:S(2)}) collective-permute-start(f32[2,1,64,512]{3,2,1,0:T(8,128)S(1)} %get-tuple-element.59), channel_id=1, source_target_pairs={{4,0},{8,4},{12,8},{16,12},{20,16},{24,20},{28,24},{5,1},{9,5},{13... | collective-permute-start | bytes 786440 | tf_op jit(solution)/shard_map/ppermute | solution.py:22
  24.8 7.7 %collective-permute-start.5 = (f32[2,1,64,512]{3,2,1,0:T(8,128)S(1)}, f32[2,1,64,512]{3,2,1,0:T(8,128)S(1)}, u32[]{:S(2)}, u32[]{:S(2)}) collective-permute-start(f32[2,1,64,512]{3,2,1,0:T(8,128)S(1)} %get-tuple-element.58), channel_id=1, source_target_pairs={{0,4},{4,8},{8,12},{12,16},{16,20},{20,24},{24,28},{1,5},{5,9},{9,... | collective-permute-start | bytes 786440 | tf_op jit(solution)/shard_map/ppermute | solution.py:20
  34.5 6.6 %collective-permute-start.7 = (f32[2,6,1,512]{3,2,1,0:T(1,128)S(1)}, f32[2,6,1,512]{3,2,1,0:T(1,128)S(1)}, u32[]{:S(2)}, u32[]{:S(2)}) collective-permute-start(f32[2,6,1,512]{3,2,1,0:T(1,128)S(1)} %get-tuple-element.42), channel_id=1, source_target_pairs={{0,1},{1,2},{2,3},{4,5},{5,6},{6,7},{8,9},{9,10},{10,11},{12,13},{... | collective-permute-start | bytes 73736 | tf_op jit(solution)/shard_map/ppermute | solution.py:20
  45.5 7.7 %collective-permute-start.9 = (f32[2,1,64,512]{3,2,1,0:T(8,128)S(1)}, f32[2,1,64,512]{3,2,1,0:T(8,128)S(1)}, u32[]{:S(2)}, u32[]{:S(2)}) collective-permute-start(f32[2,1,64,512]{3,2,1,0:T(8,128)S(1)} %get-tuple-element.56), channel_id=1, source_target_pairs={{0,4},{4,8},{8,12},{12,16},{16,20},{20,24},{24,28},{1,5},{5,9},{9,... | collective-permute-start | bytes 786440 | tf_op jit(solution)/shard_map/ppermute | solution.py:20
  55.2 6.6 %collective-permute-start.11 = (f32[2,6,1,512]{3,2,1,0:T(1,128)S(1)}, f32[2,6,1,512]{3,2,1,0:T(1,128)S(1)}, u32[]{:S(2)}, u32[]{:S(2)}) collective-permute-start(f32[2,6,1,512]{3,2,1,0:T(1,128)S(1)} %get-tuple-element.40), channel_id=1, source_target_pairs={{0,1},{1,2},{2,3},{4,5},{5,6},{6,7},{8,9},{9,10},{10,11},{12,13},{... | collective-permute-start | bytes 73736 | tf_op jit(solution)/shard_map/ppermute | solution.py:20
  82.9 7.5 %collective-permute-start.14 = (f32[2,1,64,512]{3,2,1,0:T(8,128)S(1)}, f32[2,1,64,512]{3,2,1,0:T(8,128)S(1)}, u32[]{:S(2)}, u32[]{:S(2)}) collective-permute-start(f32[2,1,64,512]{3,2,1,0:T(8,128)S(1)} %get-tuple-element.55), channel_id=1, source_target_pairs={{4,0},{8,4},{12,8},{16,12},{20,16},{24,20},{28,24},{5,1},{9,5},{13... | collective-permute-start | bytes 786440 | tf_op jit(solution)/shard_map/ppermute | solution.py:22
  86.5 7.7 %collective-permute-start.15 = (f32[2,1,64,512]{3,2,1,0:T(8,128)S(1)}, f32[2,1,64,512]{3,2,1,0:T(8,128)S(1)}, u32[]{:S(2)}, u32[]{:S(2)}) collective-permute-start(f32[2,1,64,512]{3,2,1,0:T(8,128)S(1)} %get-tuple-element.54), channel_id=1, source_target_pairs={{0,4},{4,8},{8,12},{12,16},{16,20},{20,24},{24,28},{1,5},{5,9},{9,... | collective-permute-start | bytes 786440 | tf_op jit(solution)/shard_map/ppermute | solution.py:20
  97.8 6.6 %collective-permute-start.17 = (f32[2,6,1,512]{3,2,1,0:T(1,128)S(1)}, f32[2,6,1,512]{3,2,1,0:T(1,128)S(1)}, u32[]{:S(2)}, u32[]{:S(2)}) collective-permute-start(f32[2,6,1,512]{3,2,1,0:T(1,128)S(1)} %get-tuple-element.38), channel_id=1, source_target_pairs={{0,1},{1,2},{2,3},{4,5},{5,6},{6,7},{8,9},{9,10},{10,11},{12,13},{... | collective-permute-start | bytes 73736 | tf_op jit(solution)/shard_map/ppermute | solution.py:20
  108.8 7.7 %collective-permute-start.19 = (f32[2,1,64,512]{3,2,1,0:T(8,128)S(1)}, f32[2,1,64,512]{3,2,1,0:T(8,128)S(1)}, u32[]{:S(2)}, u32[]{:S(2)}) collective-permute-start(f32[2,1,64,512]{3,2,1,0:T(8,128)S(1)} %get-tuple-element.52), channel_id=1, source_target_pairs={{0,4},{4,8},{8,12},{12,16},{16,20},{20,24},{24,28},{1,5},{5,9},{9,... | collective-permute-start | bytes 786440 | tf_op jit(solution)/shard_map/ppermute | solution.py:20
  118.5 6.6 %collective-permute-start.21 = (f32[2,6,1,512]{3,2,1,0:T(1,128)S(1)}, f32[2,6,1,512]{3,2,1,0:T(1,128)S(1)}, u32[]{:S(2)}, u32[]{:S(2)}) collective-permute-start(f32[2,6,1,512]{3,2,1,0:T(1,128)S(1)} %get-tuple-element.36), channel_id=1, source_target_pairs={{0,1},{1,2},{2,3},{4,5},{5,6},{6,7},{8,9},{9,10},{10,11},{12,13},{... | collective-permute-start | bytes 73736 | tf_op jit(solution)/shard_map/ppermute | solution.py:20
  170.3 6.3 %collective-permute-start.23 = (f32[1,512]{1,0:T(1,128)S(1)}, f32[1,512]{1,0:T(1,128)S(1)}, u32[]{:S(2)}, u32[]{:S(2)}) collective-permute-start(f32[1,512]{1,0:T(1,128)S(1)} %slice.583), channel_id=1, source_target_pairs={{4,0},{8,4},{12,8},{16,12},{20,16},{24,20},{28,24},{5,1},{9,5},{13... | collective-permute-start | bytes 6152 | tf_op jit(solution)/shard_map/ppermute | solution.py:32
  177.8 7.5 %collective-permute-start.24 = (f32[2,1,64,512]{3,2,1,0:T(8,128)S(1)}, f32[2,1,64,512]{3,2,1,0:T(8,128)S(1)}, u32[]{:S(2)}, u32[]{:S(2)}) collective-permute-start(f32[2,1,64,512]{3,2,1,0:T(8,128)S(1)} %get-tuple-element.51), channel_id=1, source_target_pairs={{4,0},{8,4},{12,8},{16,12},{20,16},{24,20},{28,24},{5,1},{9,5},{13... | collective-permute-start | bytes 786440 | tf_op jit(solution)/shard_map/ppermute | solution.py:22
  181.5 7.7 %collective-permute-start.25 = (f32[2,1,64,512]{3,2,1,0:T(8,128)S(1)}, f32[2,1,64,512]{3,2,1,0:T(8,128)S(1)}, u32[]{:S(2)}, u32[]{:S(2)}) collective-permute-start(f32[2,1,64,512]{3,2,1,0:T(8,128)S(1)} %get-tuple-element.50), channel_id=1, source_target_pairs={{0,4},{4,8},{8,12},{12,16},{16,20},{20,24},{24,28},{1,5},{5,9},{9,... | collective-permute-start | bytes 786440 | tf_op jit(solution)/shard_map/ppermute | solution.py:20
  192.7 6.6 %collective-permute-start.27 = (f32[2,6,1,512]{3,2,1,0:T(1,128)S(1)}, f32[2,6,1,512]{3,2,1,0:T(1,128)S(1)}, u32[]{:S(2)}, u32[]{:S(2)}) collective-permute-start(f32[2,6,1,512]{3,2,1,0:T(1,128)S(1)} %get-tuple-element.34), channel_id=1, source_target_pairs={{0,1},{1,2},{2,3},{4,5},{5,6},{6,7},{8,9},{9,10},{10,11},{12,13},{... | collective-permute-start | bytes 73736 | tf_op jit(solution)/shard_map/ppermute | solution.py:20
  203.8 7.7 %collective-permute-start.29 = (f32[2,1,64,512]{3,2,1,0:T(8,128)S(1)}, f32[2,1,64,512]{3,2,1,0:T(8,128)S(1)}, u32[]{:S(2)}, u32[]{:S(2)}) collective-permute-start(f32[2,1,64,512]{3,2,1,0:T(8,128)S(1)} %get-tuple-element.48), channel_id=1, source_target_pairs={{0,4},{4,8},{8,12},{12,16},{16,20},{20,24},{24,28},{1,5},{5,9},{9,... | collective-permute-start | bytes 786440 | tf_op jit(solution)/shard_map/ppermute | solution.py:20
  213.4 6.6 %collective-permute-start.31 = (f32[2,6,1,512]{3,2,1,0:T(1,128)S(1)}, f32[2,6,1,512]{3,2,1,0:T(1,128)S(1)}, u32[]{:S(2)}, u32[]{:S(2)}) collective-permute-start(f32[2,6,1,512]{3,2,1,0:T(1,128)S(1)} %get-tuple-element.32), channel_id=1, source_target_pairs={{0,1},{1,2},{2,3},{4,5},{5,6},{6,7},{8,9},{9,10},{10,11},{12,13},{... | collective-permute-start | bytes 73736 | tf_op jit(solution)/shard_map/ppermute | solution.py:20
  255.0 7.5 %collective-permute-start.34 = (f32[2,1,64,512]{3,2,1,0:T(8,128)S(1)}, f32[2,1,64,512]{3,2,1,0:T(8,128)S(1)}, u32[]{:S(2)}, u32[]{:S(2)}) collective-permute-start(f32[2,1,64,512]{3,2,1,0:T(8,128)S(1)} %get-tuple-element.47), channel_id=1, source_target_pairs={{4,0},{8,4},{12,8},{16,12},{20,16},{24,20},{28,24},{5,1},{9,5},{13... | collective-permute-start | bytes 786440 | tf_op jit(solution)/shard_map/ppermute | solution.py:22
  258.7 7.7 %collective-permute-start.35 = (f32[2,1,64,512]{3,2,1,0:T(8,128)S(1)}, f32[2,1,64,512]{3,2,1,0:T(8,128)S(1)}, u32[]{:S(2)}, u32[]{:S(2)}) collective-permute-start(f32[2,1,64,512]{3,2,1,0:T(8,128)S(1)} %get-tuple-element.46), channel_id=1, source_target_pairs={{0,4},{4,8},{8,12},{12,16},{16,20},{20,24},{24,28},{1,5},{5,9},{9,... | collective-permute-start | bytes 786440 | tf_op jit(solution)/shard_map/ppermute | solution.py:20
  269.9 6.6 %collective-permute-start.37 = (f32[2,6,1,512]{3,2,1,0:T(1,128)S(1)}, f32[2,6,1,512]{3,2,1,0:T(1,128)S(1)}, u32[]{:S(2)}, u32[]{:S(2)}) collective-permute-start(f32[2,6,1,512]{3,2,1,0:T(1,128)S(1)} %get-tuple-element.30), channel_id=1, source_target_pairs={{0,1},{1,2},{2,3},{4,5},{5,6},{6,7},{8,9},{9,10},{10,11},{12,13},{... | collective-permute-start | bytes 73736 | tf_op jit(solution)/shard_map/ppermute | solution.py:20
  283.6 8.0 %collective-permute-start.39 = (f32[2,1,64,512]{3,2,1,0:T(8,128)}, f32[2,1,64,512]{3,2,1,0:T(8,128)}, u32[]{:S(2)}, u32[]{:S(2)}) collective-permute-start(f32[2,1,64,512]{3,2,1,0:T(8,128)} %get-tuple-element.44), channel_id=1, source_target_pairs={{0,4},{4,8},{8,12},{12,16},{16,20},{20,24},{24,28},{1,5},{5,9},{9,... | collective-permute-start | bytes 786440 | tf_op jit(solution)/shard_map/ppermute | solution.py:20
  292.7 6.6 %collective-permute-start.40 = (f32[2,6,1,512]{3,2,1,0:T(1,128)S(1)}, f32[2,6,1,512]{3,2,1,0:T(1,128)S(1)}, u32[]{:S(2)}, u32[]{:S(2)}) collective-permute-start(f32[2,6,1,512]{3,2,1,0:T(1,128)S(1)} %get-tuple-element.29), channel_id=1, source_target_pairs={{1,0},{2,1},{3,2},{5,4},{6,5},{7,6},{9,8},{10,9},{11,10},{13,12},{... | collective-permute-start | bytes 73736 | tf_op jit(solution)/shard_map/ppermute | solution.py:22
  294.7 6.6 %collective-permute-start.41 = (f32[2,6,1,512]{3,2,1,0:T(1,128)S(1)}, f32[2,6,1,512]{3,2,1,0:T(1,128)S(1)}, u32[]{:S(2)}, u32[]{:S(2)}) collective-permute-start(f32[2,6,1,512]{3,2,1,0:T(1,128)S(1)} %get-tuple-element.28), channel_id=1, source_target_pairs={{0,1},{1,2},{2,3},{4,5},{5,6},{6,7},{8,9},{9,10},{10,11},{12,13},{... | collective-permute-start | bytes 73736 | tf_op jit(solution)/shard_map/ppermute | solution.py:20
  (34 other events, 292.4 us)
